TPU v7x, 768 devices: a whole 4x8x12 slice. The times are simulated.
768 devices in a mesh: seq: 64 (over y, x, core), head: 12 (over z).
Axes of the slice: x: 4, y: 8, z: 12, core: 2. Of those that a mesh axis runs over, the one named last changes fastest.
Arguments:
- queries: float32 [32768, 3072], P('seq', 'head'), may hold values from -6 to 6
- keys: float32 [32768, 3072], P('seq', 'head'), may hold values from -6 to 6
- values: float32 [32768, 3072], P('seq', 'head'), may hold values from -60 to 60
- cotangent: float32 [32768, 3072], P('seq', 'head'), may hold values from -6 to 6
- gain: float32 [3072], P('head'), may hold values from 0.1 to 1.9
Outputs:
- grad_queries: float32 [32768, 3072], P('seq', 'head')
- grad_keys: float32 [32768, 3072], P('seq', 'head')
- grad_values: float32 [32768, 3072], P('seq', 'head')
All inputs are finite; a program needn't handle non-finite values.
Results may differ from a plain program's by a relative error of at most 0.0001.
Values sent between devices are 32-bit elements; how exact they have to be, the bound alone decides.
A program may use at most 64 MiB of HBM per device.

v0:
```python
import jax
import jax.numpy as jnp
from jax import lax
from jax.sharding import PartitionSpec as P

HD = 128


def carried_in(part, axis, combine, identity, reverse):
    count = lax.axis_size(axis)
    place = lax.axis_index(axis)
    ahead = count - 1 - place if reverse else place
    gathered = lax.all_gather(part, axis)
    state = jnp.zeros_like(part) + jnp.asarray(identity, part.dtype)

    def one(hop, state):
        source = count - 1 - hop if reverse else hop
        return combine(state, lax.dynamic_index_in_dim(gathered, source, 0, False))

    return lax.fori_loop(0, ahead, one, state)


def product(form, left, right):
    return jnp.einsum(form, left, right, precision=lax.Precision.HIGHEST)


def to_blocks(array, block):
    tok_rows, width_here = array.shape
    return array.reshape(tok_rows // block, block, width_here // HD, HD).transpose(0, 2, 1, 3)


def from_blocks(array):
    count, heads_here, block, head_size = array.shape
    return array.transpose(0, 2, 1, 3).reshape(count * block, heads_here * head_size)


def add_states(earlier, later):
    return earlier + later


def shards(queries, keys, values, cotangent, gain):
    tok_rows, width_here = queries.shape
    block = min(512, tok_rows)
    query_blocks = to_blocks(queries, block)
    key_blocks = to_blocks(keys, block)
    value_blocks = to_blocks(values, block)
    causal = (jnp.arange(block)[:, None] >= jnp.arange(block)[None, :]).astype(jnp.float32)
    block_states = product("nhsd,nhse->nhde", key_blocks, value_blocks)
    own_total = jnp.sum(block_states, axis=0)
    incoming = carried_in(own_total, "seq", add_states, jnp.zeros_like(own_total), False)
    state_before = incoming[None] + jnp.cumsum(block_states, axis=0) - block_states
    scores = product("nhtd,nhsd->nhts", query_blocks, key_blocks) * causal
    attended = product("nhts,nhse->nhte", scores, value_blocks) + product(
        "nhtd,nhde->nhte", query_blocks, state_before
    )
    attended_rows = from_blocks(attended)
    scaled_cot = gain[None, :] * cotangent
    squares_part = jnp.sum(attended_rows * attended_rows, axis=1)
    cross_part = jnp.sum(scaled_cot * attended_rows, axis=1)
    squares_sum, cross_sum = lax.psum((squares_part, cross_part), "head")
    full_width = width_here * lax.axis_size("head")
    inverse = lax.rsqrt(squares_sum / full_width + 1e-06)
    cross = cross_sum / full_width
    grad_rows = (
        inverse[:, None] * scaled_cot
        - attended_rows * (inverse * inverse * inverse * cross)[:, None]
    )
    grad_blocks = to_blocks(grad_rows, block)
    grad_states = product("nhtd,nhte->nhde", query_blocks, grad_blocks)
    grad_own = jnp.sum(grad_states, axis=0)
    later_sum = carried_in(grad_own, "seq", add_states, jnp.zeros_like(grad_own), True)
    state_after = later_sum[None] + (grad_own[None] - jnp.cumsum(grad_states, axis=0))
    mixing = product("nhte,nhse->nhts", grad_blocks, value_blocks) * causal
    grad_q = product("nhts,nhsd->nhtd", mixing, key_blocks) + product(
        "nhde,nhte->nhtd", state_before, grad_blocks
    )
    grad_k = product("nhts,nhtd->nhsd", mixing, query_blocks) + product(
        "nhde,nhse->nhsd", state_after, value_blocks
    )
    grad_v = product("nhts,nhte->nhse", scores, grad_blocks) + product(
        "nhde,nhsd->nhse", state_after, key_blocks
    )
    return (from_blocks(grad_q), from_blocks(grad_k), from_blocks(grad_v))


def solution(mesh):
    in_specs = (P("seq", "head"), P("seq", "head"), P("seq", "head"), P("seq", "head"), P("head"))
    out_specs = (P("seq", "head"), P("seq", "head"), P("seq", "head"))
    return jax.shard_map(shards, mesh=mesh, in_specs=in_specs, out_specs=out_specs, check_vma=False)
```

profile of v0, /device:TPU:1, one launch (start us, length us, event | category | flops | bytes accessed | tf_op | source)
XLA Modules:
  0.0 380.6 jit_solution(8679964364682491374)
XLA Ops:
  7.2 1.3 reshape.118
  8.6 1.5 reshape.120
  10.1 1.7 fusion.32
  11.9 1.1 reshape.116
  13.0 3.0 fusion.29
  16.1 98.1 %all-gather.5.cloned.1.call-done = f32[128,128,128]{2,1,0:T(8,128)} async-done(((f32[2,128,128]{2,1,0:T(8,128)}), f32[128,128,128]{2,1,0:T(8,128)}) %all-gather.5.cloned.1.call-update) | async-done | bytes 8388624 | tf_op jit(solution)/shard_map/all_gather | solution.py:13
  114.2 1.0 while.22
  114.2 0.9 bitcast_add_fusion.4
  115.2 1.7 convolution_bitcast_fusion.2
  116.9 4.2 %fusion.25 = (f32[512]{0:T(512)S(1)}, f32[2,512,128]{1,2,0:T(8,128)}) fusion(f32[2,512,128]{1,2,0:T(8,128)S(1)} %convolution_bitcast_fusion.2, f32[1,512,2,128]{3,2,1,0:T(2,128)} %copy-done.1, f32[2,512,512]{2,1,0:T(8,128)S(1)} %fusion.29, f32[512,512]{1,0:T(8,128)S(1)} %fusion.24), kind=kOutput, calls=%fused_computation.25 | convolution fusion | flops 806223360 | bytes 4720640 | tf_op jit(solution)/shard_map/nhts,nhse->nhte/dot_general | solution.py:24
  121.1 2.0 copy.34
  123.1 1.3 multiply_reduce_fusion
  124.5 20.0 %all-reduce = (f32[512]{0:T(512)S(1)}, f32[512]{0:T(512)S(1)}) all-reduce(f32[512]{0:T(512)S(1)} %multiply_reduce_fusion, f32[512]{0:T(512)S(1)} %get-tuple-element.114), channel_id=1, replica_groups=mesh['seq'=64,'head'=12] {'head'}, use_global_device_ids=true, to_apply=%region_5.6 | all-reduce | flops 1024 | bytes 8192 | tf_op jit(solution)/shard_map/psum | solution.py:60
  144.5 2.2 multiply_subtract_fusion
  146.7 2.0 copy.58
  148.7 1.8 convolution_bitcast_fusion.3
  151.4 1.7 fusion.53
  153.1 3.0 fusion.36
  156.1 3.2 fusion.14
  159.4 2.0 copy.43
  161.4 140.0 %all-gather.7.cloned.1.call-done = f32[128,128,128]{2,1,0:T(8,128)} async-done(((f32[2,128,128]{2,1,0:T(8,128)}), f32[128,128,128]{2,1,0:T(8,128)}) %all-gather.7.cloned.1.call-update) | async-done | bytes 8388624 | tf_op jit(solution)/shard_map/all_gather | solution.py:13
  301.4 59.5 %while.23 = (s32[]{:T(128)}, f32[2,128,128]{2,1,0:T(8,128)S(1)}, s32[]{:T(128)}, f32[64,2,128,128]{3,2,1,0:T(8,128)}, s32[]{:T(128)}, /*index=5*/s32[]{:T(128)}, s32[]{:T(128)}, s32[]{:T(128)}) while((s32[]{:T(128)}, f32[2,128,128]{2,1,0:T(8,128)S(1)}, s32[]{:T(128)}, f32[64,2,128,128]{3,2,1,0:T(8,128)}, s32[]{:T(128)}, /*index=5*/s32[]{:T(128)}, ...), condition=%wide.region_7.8_spmd, body=%wide.region_6.7_spmd.sunk | while | flops 32774 | bytes 393359 | solution.py:20
  301.4 0.9 bitcast_add_fusion.5
  302.4 0.9 bitcast_add_fusion.5
  303.3 0.9 bitcast_add_fusion.5
  304.3 0.9 bitcast_add_fusion.5
  305.2 0.9 bitcast_add_fusion.5
  306.2 0.9 bitcast_add_fusion.5
  307.2 0.9 bitcast_add_fusion.5
  308.1 0.9 bitcast_add_fusion.5
  309.1 0.9 bitcast_add_fusion.5
  310.0 0.9 bitcast_add_fusion.5
  311.0 0.9 bitcast_add_fusion.5
  312.0 0.9 bitcast_add_fusion.5
  312.9 0.9 bitcast_add_fusion.5
  313.9 0.9 bitcast_add_fusion.5
  314.8 0.9 bitcast_add_fusion.5
  315.8 0.9 bitcast_add_fusion.5
  316.8 0.9 bitcast_add_fusion.5
  317.7 0.9 bitcast_add_fusion.5
  318.7 0.9 bitcast_add_fusion.5
  319.6 0.9 bitcast_add_fusion.5
  320.6 0.9 bitcast_add_fusion.5
  321.6 0.9 bitcast_add_fusion.5
  322.5 0.9 bitcast_add_fusion.5
  323.5 0.9 bitcast_add_fusion.5
  324.4 0.9 bitcast_add_fusion.5
  325.4 0.9 bitcast_add_fusion.5
  326.3 0.9 bitcast_add_fusion.5
  327.3 0.9 bitcast_add_fusion.5
  328.3 0.9 bitcast_add_fusion.5
  329.2 0.9 bitcast_add_fusion.5
  330.2 0.9 bitcast_add_fusion.5
  331.1 0.9 bitcast_add_fusion.5
  332.1 0.9 bitcast_add_fusion.5
  333.1 0.9 bitcast_add_fusion.5
  344.6 0.9 bitcast_add_fusion.5
  347.5 0.9 bitcast_add_fusion.5
  361.0 1.7 convolution_bitcast_fusion
  362.7 2.5 convolution_bitcast_fusion.1
  365.2 2.2 fusion.11
  367.4 2.0 copy.45
  369.4 3.3 fusion.17
  372.8 1.0 copy.44
  (52 shorter events, 25.5 us)
Async XLA Ops:
  7.2 4.7 %copy-start.6 = (f32[512,256]{1,0:T(8,128)S(1)}, f32[512,256]{1,0:T(8,128)}, u32[]{:S(2)}) copy-start(f32[512,256]{1,0:T(8,128)} %param.9) | copy-start | bytes 1572868
  7.2 107.0 %all-gather.5.cloned.1.call-start = ((), (), s32[]{:S(2)}) async-start(), calls=%async_computation | async-start | bytes 8519680 | tf_op jit(solution)/shard_map/all_gather | solution.py:13
  8.6 3.3 copy-start.2
  10.1 1.8 copy-start.1
  11.8 289.6 %all-gather.7.cloned.1.call-start = ((), (), s32[]{:S(2)}) async-start(), calls=%async_computation.1 | async-start | bytes 8519680 | tf_op jit(solution)/shard_map/all_gather | solution.py:13
  13.0 102.1 %copy-start.5 = (f32[2,128,128]{2,1,0:T(8,128)S(1)}, f32[2,128,128]{2,1,0:T(8,128)}, u32[]{:S(2)}) copy-start(f32[2,128,128]{2,1,0:T(8,128)} %fusion.32) | copy-start | bytes 393220
  116.9 6.3 %copy-start.7 = (f32[256]{0:T(256)S(1)}, f32[256]{0:T(256)}, u32[]{:S(2)}) copy-start(f32[256]{0:T(256)} %param.13) | copy-start | bytes 3076
  151.4 4.8 %copy-start.3 = (f32[1,512,2,128]{3,2,1,0:T(2,128)S(1)}, f32[1,512,2,128]{3,2,1,0:T(2,128)}, u32[]{:S(2)}) copy-start(f32[1,512,2,128]{3,2,1,0:T(2,128)} %copy-done.2) | copy-start | bytes 1572868
  156.1 3.3 copy-start
  361.0 4.2 %copy-start.4 = (f32[512,256]{0,1:T(8,128)S(1)}, f32[512,256]{0,1:T(8,128)}, u32[]{:S(2)}) copy-start(f32[512,256]{0,1:T(8,128)} %copy.58) | copy-start | bytes 1572868
Sparse Core Ops, SparseCore 0:
  12.5 101.6 all-gather.4
  151.5 149.8 all-gather.6
where the time goes:
time: 382 us; the launch traced here: 381 us
  waiting for transfers between devices  238 us (62%)
  other arithmetic  62.7 us (16%)
  matrix products  30.1 us (8%)
  blocking collectives  20 us (5%)
  between operations  14.2 us (4%)
  local copies, waits for them, and re-layouts  13.9 us (4%)
    all_gather x2, waiting for transfers between devices, carried_in(): gathered = lax.all_gather(part, axis)  238 us
    add x63, other arithmetic, add_states(): return earlier + later  59 us
    dot_general x12, matrix products, product(): return jnp.einsum(form, left, right, precision=lax.Precision.HIGHEST)  30.1 us
    psum x1, blocking collectives, shards(): squares_sum, cross_sum = lax.psum((squares_part, cross_part), 'head')  20 us
  transfers between devices with their start and end apart: 2, of which 2 were waited for; matrix products, arithmetic and copies ran while one was open for 4% of the time, Pallas kernels for 0%

commit v1 on v0

v1 whole, which is shorter than its diff:
```python
import functools

import jax
import jax.numpy as jnp
from jax import lax
from jax.experimental import pallas as pl
from jax.experimental.pallas import tpu as pltpu
from jax.sharding import PartitionSpec as P

HD = 128
ROW = 8
CHUNK = 256
EPS = 1e-06
MESH = pl.DeviceIdType.MESH
F32 = jnp.float32
BF16 = jnp.bfloat16


def split(x):
    high = x.astype(BF16)
    return high, (x - high.astype(F32)).astype(BF16)


def dot3(left, right, dims):
    def one(a, b):
        return lax.dot_general(a, b, (dims, ((), ())), preferred_element_type=F32)

    (lh, ll), (rh, rl) = left, right
    return one(lh, rh) + (one(lh, rl) + one(ll, rh))


NN = ((1,), (0,))
NT = ((1,), (1,))
TN = ((0,), (0,))


def body(
    n_seq,
    n_head,
    q_hbm,
    k_hbm,
    v_hbm,
    cot_hbm,
    gain_ref,
    gq_hbm,
    gk_hbm,
    gv_hbm,
    q_s,
    k_s,
    v_s,
    sc_s,
    att_s,
    gq_s,
    gk_s,
    gv_s,
    qh,
    ql,
    kh,
    kl,
    vh,
    vl,
    gh,
    gl,
    sco_h,
    sco_l,
    bd_h,
    bd_l,
    own,
    row_in,
    col_in,
    row_out,
    state,
    norm_own,
    norm_in,
    in_sem,
    out_sem,
    send_sem,
    recv_sem,
):
    n_y = n_seq // ROW
    tokens, width = q_s.shape
    heads = width // HD
    chunks = tokens // CHUNK
    part = heads * HD // ROW
    s = lax.axis_index("seq")
    h = lax.axis_index("head")
    j = lax.rem(s, ROW)
    y = lax.div(s, ROW)

    def row_peer(k):
        return (y * ROW + lax.rem(j + k, ROW), h)

    def col_peer(m):
        return (lax.rem(y + m, n_y) * ROW + j, h)

    def head_peer(m):
        return (s, lax.rem(h + m, n_head))

    loads = [
        pltpu.make_async_copy(src, dst, in_sem.at[i])
        for i, (src, dst) in enumerate(
            [(k_hbm, k_s), (v_hbm, v_s), (q_hbm, q_s), (cot_hbm, sc_s)]
        )
    ]
    for load in loads:
        load.start()
    barrier = pltpu.get_barrier_semaphore()
    peers = (
        [row_peer(k) for k in range(1, ROW)]
        + [col_peer(m) for m in range(1, n_y)]
        + [head_peer(m) for m in range(1, n_head)]
    )
    for peer in peers:
        pl.semaphore_signal(barrier, inc=1, device_id=peer, device_id_type=MESH)

    def send(src, dst, stage, peer):
        pltpu.make_async_remote_copy(
            src_ref=src,
            dst_ref=dst,
            send_sem=send_sem.at[stage],
            recv_sem=recv_sem.at[stage],
            device_id=peer,
            device_id_type=MESH,
        ).start()

    def wait_in(ref, stage):
        pltpu.make_async_remote_copy(
            src_ref=ref,
            dst_ref=ref,
            send_sem=send_sem.at[stage],
            recv_sem=recv_sem.at[stage],
            device_id=row_peer(1),
            device_id_type=MESH,
        ).wait_recv()

    def wait_out(ref, stage):
        pltpu.make_async_remote_copy(
            src_ref=ref,
            dst_ref=ref,
            send_sem=send_sem.at[stage],
            recv_sem=recv_sem.at[stage],
            device_id=row_peer(1),
            device_id_type=MESH,
        ).wait_send()

    def weight(cond):
        return jnp.where(cond, 1.0, 0.0).astype(F32)

    def scan_row(scan):
        for k in range(1, ROW):
            there = lax.rem(j + k, ROW)
            send(
                own.at[scan, pl.ds(pl.multiple_of(there * part, part), part)],
                row_in.at[scan, k - 1],
                3 * scan,
                row_peer(k),
            )

    def scan_col(scan):
        wait_in(row_in.at[scan], 3 * scan)
        total = own[scan, pl.ds(pl.multiple_of(j * part, part), part)]
        for k in range(1, ROW):
            total = total + row_in[scan, k - 1]
        col_in[scan, n_y - 1] = total
        for m in range(1, n_y):
            send(
                col_in.at[scan, n_y - 1],
                col_in.at[scan, m - 1],
                3 * scan + 1,
                col_peer(m),
            )

    def scan_back(scan):
        if n_y > 1:
            wait_in(col_in.at[scan, pl.ds(0, n_y - 1)], 3 * scan + 1)
        base = jnp.zeros((part, HD), F32)
        for m in range(1, n_y):
            inside = (y < m) if scan else (y >= m)
            base = base + weight(inside) * col_in[scan, m - 1]
        mine = own[scan, pl.ds(pl.multiple_of(j * part, part), part)]
        for k in range(ROW):
            there = lax.rem(j + k, ROW)
            value = base
            for r in range(ROW):
                source = lax.rem(j - r + ROW, ROW)
                inside = (source > there) if scan else (source < there)
                piece = mine if r == 0 else row_in[scan, r - 1]
                if r != k or k == 0:
                    pass
                value = value + weight(inside) * piece
            if k == 0:
                state[scan, pl.ds(pl.multiple_of(j * part, part), part)] = value
            else:
                row_out[scan, k - 1] = value
                send(
                    row_out.at[scan, k - 1],
                    state.at[scan, pl.ds(pl.multiple_of(j * part, part), part)],
                    3 * scan + 2,
                    row_peer(k),
                )

    def scan_end(scan):
        wait_in(state.at[scan, pl.ds(0, (ROW - 1) * part)], 3 * scan + 2)

    def cols(head):
        return slice(head * HD, (head + 1) * HD)

    def rows(chunk):
        return slice(chunk * CHUNK, (chunk + 1) * CHUNK)

    def diagonal(full):
        return jnp.concatenate([full[cols(i), cols(i)] for i in range(heads)], axis=0)

    def put_block_diagonal(slot, stacked):
        high, low = split(stacked)
        for i in range(heads):
            bd_h[slot, cols(i), cols(i)] = high[cols(i)]
            bd_l[slot, cols(i), cols(i)] = low[cols(i)]

    def pair(high, low, *index):
        return high[index], low[index]

    bd_h[...] = jnp.zeros_like(bd_h)
    bd_l[...] = jnp.zeros_like(bd_l)
    lower = lax.broadcasted_iota(jnp.int32, (CHUNK, CHUNK), 0) >= lax.broadcasted_iota(
        jnp.int32, (CHUNK, CHUNK), 1
    )

    loads[0].wait()
    kh[...], kl[...] = split(k_s[...])
    loads[1].wait()
    vh[...], vl[...] = split(v_s[...])
    total = jnp.zeros((heads * HD, HD), F32)
    for c in range(chunks):
        here = diagonal(dot3(pair(kh, kl, rows(c)), pair(vh, vl, rows(c)), TN))
        total = total + here
        if c + 1 < chunks:
            put_block_diagonal(c, total)
    own[0] = total
    pl.semaphore_wait(barrier, len(peers))
    scan_row(0)

    loads[2].wait()
    qh[...], ql[...] = split(q_s[...])
    for c in range(chunks):
        for i in range(heads):
            scores = dot3(
                pair(qh, ql, rows(c), cols(i)), pair(kh, kl, rows(c), cols(i)), NT
            )
            sco_h[c, i], sco_l[c, i] = split(jnp.where(lower, scores, 0.0))
    loads[3].wait()
    sc_s[...] = sc_s[...] * gain_ref[...]
    scan_col(0)
    for c in range(chunks):
        for i in range(heads):
            inner = dot3(pair(sco_h, sco_l, c, i), pair(vh, vl, rows(c), cols(i)), NN)
            att_s[rows(c), cols(i)] = inner
        if c > 0:
            att_s[rows(c)] += dot3(
                pair(qh, ql, rows(c)), pair(bd_h, bd_l, c - 1), NN
            )
    scan_back(0)
    scan_end(0)

    put_block_diagonal(chunks, state[0])
    lane = lax.broadcasted_iota(jnp.int32, (HD, HD), 1)
    groups = tokens // HD
    sums = jnp.zeros((HD, HD), F32)
    att = att_s[...] + dot3((qh[...], ql[...]), pair(bd_h, bd_l, chunks), NN)
    att_s[...] = att
    squares = jnp.sum(att * att, axis=1, keepdims=True)
    cross = jnp.sum(att * sc_s[...], axis=1, keepdims=True)
    for g in range(groups):
        piece = slice(g * HD, (g + 1) * HD)
        sums = jnp.where(lane == g, squares[piece], sums)
        sums = jnp.where(lane == groups + g, cross[piece], sums)
    norm_own[...] = sums.T[: 2 * groups]
    for m in range(1, n_head):
        send(norm_own, norm_in.at[m - 1], 6, head_peer(m))
    both = norm_own[...]
    if n_head > 1:
        wait_in(norm_in, 6)
        for m in range(1, n_head):
            both = both + norm_in[m - 1]
    mean = both / (width * n_head)
    inverse = lax.rsqrt(mean[:groups] + EPS)
    slope = inverse * inverse * inverse * mean[groups:]
    factors = jnp.concatenate(
        [inverse, slope, jnp.zeros((HD - 2 * groups, HD), F32)], axis=0
    ).T
    for g in range(groups):
        piece = slice(g * HD, (g + 1) * HD)
        grad = (
            factors[:, g : g + 1] * sc_s[piece]
            - factors[:, groups + g : groups + g + 1] * att_s[piece]
        )
        gh[piece], gl[piece] = split(grad)

    total = jnp.zeros((heads * HD, HD), F32)
    for c in reversed(range(chunks)):
        here = diagonal(dot3(pair(qh, ql, rows(c)), pair(gh, gl, rows(c)), TN))
        total = total + here
        if c > 0:
            put_block_diagonal(chunks + c, total)
    own[1] = total
    scan_row(1)

    def mix(c):
        for i in range(heads):
            here = (rows(c), cols(i))
            mixing = dot3(pair(gh, gl, *here), pair(vh, vl, *here), NT)
            mixing = split(jnp.where(lower, mixing, 0.0))
            gq_s[here] = dot3(mixing, pair(kh, kl, *here), NN)
            gk_s[here] = dot3(mixing, pair(qh, ql, *here), TN)
            gv_s[here] = dot3(pair(sco_h, sco_l, c, i), pair(gh, gl, *here), TN)
        gq_s[rows(c)] += dot3(pair(gh, gl, rows(c)), pair(bd_h, bd_l, chunks), NT)
        if c > 0:
            gq_s[rows(c)] += dot3(pair(gh, gl, rows(c)), pair(bd_h, bd_l, c - 1), NT)
        if c + 1 < chunks:
            after = pair(bd_h, bd_l, chunks + c + 1)
            gk_s[rows(c)] += dot3(pair(vh, vl, rows(c)), after, NT)
            gv_s[rows(c)] += dot3(pair(kh, kl, rows(c)), after, NN)

    mix(0)
    scan_col(1)
    for c in range(1, chunks):
        mix(c)
    store_q = pltpu.make_async_copy(gq_s, gq_hbm, out_sem.at[0])
    store_q.start()
    scan_back(1)
    scan_end(1)

    put_block_diagonal(2 * chunks, state[1])
    after = pair(bd_h, bd_l, 2 * chunks)
    gk_s[...] += dot3((vh[...], vl[...]), after, NT)
    store_k = pltpu.make_async_copy(gk_s, gk_hbm, out_sem.at[1])
    store_k.start()
    gv_s[...] += dot3((kh[...], kl[...]), after, NN)
    store_v = pltpu.make_async_copy(gv_s, gv_hbm, out_sem.at[2])
    store_v.start()
    for scan in range(2):
        wait_out(row_in.at[scan], 3 * scan)
        if n_y > 1:
            wait_out(col_in.at[scan, pl.ds(0, n_y - 1)], 3 * scan + 1)
        wait_out(row_out.at[scan], 3 * scan + 2)
    if n_head > 1:
        wait_out(norm_in, 6)
    store_q.wait()
    store_k.wait()
    store_v.wait()


def shards(n_seq, n_head, queries, keys, values, cotangent, gain):
    tokens, width = queries.shape
    heads = width // HD
    chunks = tokens // CHUNK
    n_y = n_seq // ROW
    part = heads * HD // ROW
    full = (tokens, width)
    norm_rows = 2 * tokens // HD
    anywhere = pl.BlockSpec(memory_space=pl.ANY)
    out = jax.ShapeDtypeStruct(full, F32)
    return tuple(
        pl.pallas_call(
            functools.partial(body, n_seq, n_head),
            out_shape=(out, out, out),
            in_specs=[anywhere] * 4 + [pl.BlockSpec(memory_space=pltpu.VMEM)],
            out_specs=(anywhere,) * 3,
            scratch_shapes=[pltpu.VMEM(full, F32)] * 8
            + [pltpu.VMEM(full, BF16)] * 8
            + [pltpu.VMEM((chunks, heads, CHUNK, CHUNK), BF16)] * 2
            + [pltpu.VMEM((2 * chunks + 1, width, width), BF16)] * 2
            + [
                pltpu.VMEM((2, heads * HD, HD), F32),
                pltpu.VMEM((2, ROW - 1, part, HD), F32),
                pltpu.VMEM((2, n_y, part, HD), F32),
                pltpu.VMEM((2, ROW - 1, part, HD), F32),
                pltpu.VMEM((2, heads * HD, HD), F32),
                pltpu.VMEM((norm_rows, HD), F32),
                pltpu.VMEM((max(n_head - 1, 1), norm_rows, HD), F32),
                pltpu.SemaphoreType.DMA((4,)),
                pltpu.SemaphoreType.DMA((3,)),
                pltpu.SemaphoreType.DMA((7,)),
                pltpu.SemaphoreType.DMA((7,)),
            ],
            compiler_params=pltpu.CompilerParams(
                collective_id=0, has_side_effects=True
            ),
        )(queries, keys, values, cotangent, gain[None, :])
    )


def solution(mesh):
    in_specs = (P("seq", "head"), P("seq", "head"), P("seq", "head"), P("seq", "head"), P("head"))
    out_specs = (P("seq", "head"), P("seq", "head"), P("seq", "head"))
    return jax.shard_map(
        functools.partial(shards, mesh.shape["seq"], mesh.shape["head"]),
        mesh=mesh,
        in_specs=in_specs,
        out_specs=out_specs,
        check_vma=False,
    )
```

time: 382 us -> 60.8 us (0.16)
  waiting for transfers between devices: 238 us -> 0 us
  other arithmetic: 62.7 us -> 0 us
  Pallas kernels: 0 us -> 56 us
  matrix products: 30.1 us -> 0 us
  blocking collectives: 20 us -> 0 us
  between operations: 14.2 us -> 0.65 us
  local copies, waits for them, and re-layouts: 13.9 us -> 3.95 us
    all_gather x2 -> x0, waiting for transfers between devices: 238 us -> none  [carried_in(): gathered = lax.all_gather(part, axis)]
    add x63 -> x0, other arithmetic: 59 us -> none  [add_states(): return earlier + later]
    pallas_call x0 -> x1, Pallas kernels: none -> 56 us  [shards(): pl.pallas_call(functools.partial(body, n_seq, n_head), out_shape=(out, ou...]
    dot_general x12 -> x0, matrix products: 30.1 us -> none  [product(): return jnp.einsum(form, left, right, precision=lax.Precision.HIGHEST)]
    psum x1 -> x0, blocking collectives: 20 us -> none  [shards(): squares_sum, cross_sum = lax.psum((squares_part, cross_part), 'head')]
    reshape x5 -> x0, local copies, waits for them, and re-layouts: 7.97 us -> none  [the longest x4 5.93 us: to_blocks(): array.reshape(tok_rows // block, block, width_here // HD, HD)]
  transfers between devices with their start and end apart: 2 -> 0, of which waited for: 2 -> 0; matrix products, arithmetic and copies ran while one was open for 4% -> 0% of each run, Pallas kernels for 0% -> 0%
where the time goes in v1:
time: 60.8 us; the launch traced here: 60.6 us
  Pallas kernels  56 us (92%)
  local copies, waits for them, and re-layouts  3.95 us (6%)
  between operations  0.65 us (1%)
    pallas_call x1, Pallas kernels, shards(): pl.pallas_call(functools.partial(body, n_seq, n_head), out_shape=(out, ou...  56 us
    unnamed x7, local copies, waits for them, and re-layouts  3.95 us

profile of v1, /device:TPU:1, one launch (start us, length us, event | category | flops | bytes accessed | tf_op | source)
XLA Modules:
  0.0 60.6 jit_solution(11740166730938291007)
XLA Ops:
  0.6 56.0 %shard_map.76 = (f32[512,256]{1,0:T(8,128)}, f32[512,256]{1,0:T(8,128)}, f32[512,256]{1,0:T(8,128)}) custom-call(f32[512,256]{1,0:T(8,128)} %q_hbm.1, f32[512,256]{1,0:T(8,128)} %k_hbm.1, f32[512,256]{1,0:T(8,128)} %v_hbm.1, f32[512,256]{1,0:T(8,128)} %cot_hbm.1, f32[1,256]{1,0:T(1,128)} %bitcast.1), custom_call_target="tpu_custom_call" | custom-call | tf_op jit(solution)/shard_map/pallas_call | solution.py:364
  56.6 0.0 copy-start.1
  56.6 1.9 %copy.11 = f32[512,256]{1,0:T(8,128)} copy(f32[512,256]{1,0:T(8,128)} %get-tuple-element.6) | data formatting | bytes 1048576
  58.5 0.0 copy-done.1
  58.5 0.0 copy-start
  58.6 0.8 %copy.12 = f32[512,256]{1,0:T(8,128)} copy(f32[512,256]{1,0:T(8,128)S(1)} %copy-done.1) | data formatting | bytes 1048576
  59.3 0.4 copy-done
  59.8 0.8 %copy.13 = f32[512,256]{1,0:T(8,128)} copy(f32[512,256]{1,0:T(8,128)S(1)} %copy-done) | data formatting | bytes 1048576
Async XLA Ops:
  56.6 1.9 %copy-start.1 = (f32[512,256]{1,0:T(8,128)S(1)}, f32[512,256]{1,0:T(8,128)}, u32[]{:S(2)}) copy-start(f32[512,256]{1,0:T(8,128)} %get-tuple-element.7) | copy-start | bytes 1572868
  58.5 1.2 %copy-start = (f32[512,256]{1,0:T(8,128)S(1)}, f32[512,256]{1,0:T(8,128)}, u32[]{:S(2)}) copy-start(f32[512,256]{1,0:T(8,128)} %get-tuple-element.8) | copy-start | bytes 1572868

commit v2 on v1

--- a/solution.py
+++ b/solution.py
@@ -27,6 +27,10 @@
 
     (lh, ll), (rh, rl) = left, right
     return one(lh, rh) + (one(lh, rl) + one(ll, rh))
+
+
+def far_first(count):
+    return sorted(range(1, count), key=lambda m: -min(m, count - m))
 
 
 NN = ((1,), (0,))
@@ -42,23 +46,22 @@
     v_hbm,
     cot_hbm,
     gain_ref,
-    gq_hbm,
-    gk_hbm,
-    gv_hbm,
+    gq_s,
+    gk_s,
+    gv_s,
+    kh,
+    kl,
+    vh,
+    vl,
+    after_h,
+    after_l,
     q_s,
     k_s,
     v_s,
     sc_s,
     att_s,
-    gq_s,
-    gk_s,
-    gv_s,
     qh,
     ql,
-    kh,
-    kl,
-    vh,
-    vl,
     gh,
     gl,
     sco_h,
@@ -73,7 +76,6 @@
     norm_own,
     norm_in,
     in_sem,
-    out_sem,
     send_sem,
     recv_sem,
 ):
@@ -147,7 +149,7 @@
         return jnp.where(cond, 1.0, 0.0).astype(F32)
 
     def scan_row(scan):
-        for k in range(1, ROW):
+        for k in far_first(ROW):
             there = lax.rem(j + k, ROW)
             send(
                 own.at[scan, pl.ds(pl.multiple_of(there * part, part), part)],
@@ -162,7 +164,7 @@
         for k in range(1, ROW):
             total = total + row_in[scan, k - 1]
         col_in[scan, n_y - 1] = total
-        for m in range(1, n_y):
+        for m in far_first(n_y):
             send(
                 col_in.at[scan, n_y - 1],
                 col_in.at[scan, m - 1],
@@ -178,15 +180,13 @@
             inside = (y < m) if scan else (y >= m)
             base = base + weight(inside) * col_in[scan, m - 1]
         mine = own[scan, pl.ds(pl.multiple_of(j * part, part), part)]
-        for k in range(ROW):
+        for k in far_first(ROW) + [0]:
             there = lax.rem(j + k, ROW)
             value = base
             for r in range(ROW):
                 source = lax.rem(j - r + ROW, ROW)
                 inside = (source > there) if scan else (source < there)
                 piece = mine if r == 0 else row_in[scan, r - 1]
-                if r != k or k == 0:
-                    pass
                 value = value + weight(inside) * piece
             if k == 0:
                 state[scan, pl.ds(pl.multiple_of(j * part, part), part)] = value
@@ -275,7 +275,7 @@
         sums = jnp.where(lane == g, squares[piece], sums)
         sums = jnp.where(lane == groups + g, cross[piece], sums)
     norm_own[...] = sums.T[: 2 * groups]
-    for m in range(1, n_head):
+    for m in far_first(n_head):
         send(norm_own, norm_in.at[m - 1], 6, head_peer(m))
     both = norm_own[...]
     if n_head > 1:
@@ -325,19 +325,15 @@
     scan_col(1)
     for c in range(1, chunks):
         mix(c)
-    store_q = pltpu.make_async_copy(gq_s, gq_hbm, out_sem.at[0])
-    store_q.start()
     scan_back(1)
     scan_end(1)
 
-    put_block_diagonal(2 * chunks, state[1])
-    after = pair(bd_h, bd_l, 2 * chunks)
-    gk_s[...] += dot3((vh[...], vl[...]), after, NT)
-    store_k = pltpu.make_async_copy(gk_s, gk_hbm, out_sem.at[1])
-    store_k.start()
-    gv_s[...] += dot3((kh[...], kl[...]), after, NN)
-    store_v = pltpu.make_async_copy(gv_s, gv_hbm, out_sem.at[2])
-    store_v.start()
+    after_h[...] = jnp.zeros_like(after_h)
+    after_l[...] = jnp.zeros_like(after_l)
+    high, low = split(state[1])
+    for i in range(heads):
+        after_h[cols(i), cols(i)] = high[cols(i)]
+        after_l[cols(i), cols(i)] = low[cols(i)]
     for scan in range(2):
         wait_out(row_in.at[scan], 3 * scan)
         if n_y > 1:
@@ -345,9 +341,23 @@
         wait_out(row_out.at[scan], 3 * scan + 2)
     if n_head > 1:
         wait_out(norm_in, 6)
-    store_q.wait()
-    store_k.wait()
-    store_v.wait()
+
+
+def finish(
+    gq_s, gk_s, gv_s, kh, kl, vh, vl, after_h, after_l, gq_hbm, gk_hbm, gv_hbm, k_out, v_out, sem
+):
+    after = (after_h[...], after_l[...])
+    stores = [
+        pltpu.make_async_copy(src, dst, sem.at[i])
+        for i, (src, dst) in enumerate([(gq_s, gq_hbm), (k_out, gk_hbm), (v_out, gv_hbm)])
+    ]
+    stores[0].start()
+    k_out[...] = gk_s[...] + dot3((vh[...], vl[...]), after, NT)
+    stores[1].start()
+    v_out[...] = gv_s[...] + dot3((kh[...], kl[...]), after, NN)
+    stores[2].start()
+    for store in stores:
+        store.wait()
 
 
 def shards(n_seq, n_head, queries, keys, values, cotangent, gain):
@@ -359,34 +369,41 @@
     full = (tokens, width)
     norm_rows = 2 * tokens // HD
     anywhere = pl.BlockSpec(memory_space=pl.ANY)
+    vmem = pl.BlockSpec(memory_space=pltpu.VMEM)
+    blocks = pl.pallas_call(
+        functools.partial(body, n_seq, n_head),
+        out_shape=(pltpu.VMEM(full, F32),) * 3
+        + (pltpu.VMEM(full, BF16),) * 4
+        + (pltpu.VMEM((width, width), BF16),) * 2,
+        in_specs=[anywhere] * 4 + [vmem],
+        out_specs=(vmem,) * 9,
+        scratch_shapes=[pltpu.VMEM(full, F32)] * 5
+        + [pltpu.VMEM(full, BF16)] * 4
+        + [pltpu.VMEM((chunks, heads, CHUNK, CHUNK), BF16)] * 2
+        + [pltpu.VMEM((2 * chunks, width, width), BF16)] * 2
+        + [
+            pltpu.VMEM((2, heads * HD, HD), F32),
+            pltpu.VMEM((2, ROW - 1, part, HD), F32),
+            pltpu.VMEM((2, n_y, part, HD), F32),
+            pltpu.VMEM((2, ROW - 1, part, HD), F32),
+            pltpu.VMEM((2, heads * HD, HD), F32),
+            pltpu.VMEM((norm_rows, HD), F32),
+            pltpu.VMEM((max(n_head - 1, 1), norm_rows, HD), F32),
+            pltpu.SemaphoreType.DMA((4,)),
+            pltpu.SemaphoreType.DMA((7,)),
+            pltpu.SemaphoreType.DMA((7,)),
+        ],
+        compiler_params=pltpu.CompilerParams(collective_id=0, has_side_effects=True),
+    )(queries, keys, values, cotangent, gain[None, :])
     out = jax.ShapeDtypeStruct(full, F32)
     return tuple(
         pl.pallas_call(
-            functools.partial(body, n_seq, n_head),
+            finish,
             out_shape=(out, out, out),
-            in_specs=[anywhere] * 4 + [pl.BlockSpec(memory_space=pltpu.VMEM)],
+            in_specs=[vmem] * 9,
             out_specs=(anywhere,) * 3,
-            scratch_shapes=[pltpu.VMEM(full, F32)] * 8
-            + [pltpu.VMEM(full, BF16)] * 8
-            + [pltpu.VMEM((chunks, heads, CHUNK, CHUNK), BF16)] * 2
-            + [pltpu.VMEM((2 * chunks + 1, width, width), BF16)] * 2
-            + [
-                pltpu.VMEM((2, heads * HD, HD), F32),
-                pltpu.VMEM((2, ROW - 1, part, HD), F32),
-                pltpu.VMEM((2, n_y, part, HD), F32),
-                pltpu.VMEM((2, ROW - 1, part, HD), F32),
-                pltpu.VMEM((2, heads * HD, HD), F32),
-                pltpu.VMEM((norm_rows, HD), F32),
-                pltpu.VMEM((max(n_head - 1, 1), norm_rows, HD), F32),
-                pltpu.SemaphoreType.DMA((4,)),
-                pltpu.SemaphoreType.DMA((3,)),
-                pltpu.SemaphoreType.DMA((7,)),
-                pltpu.SemaphoreType.DMA((7,)),
-            ],
-            compiler_params=pltpu.CompilerParams(
-                collective_id=0, has_side_effects=True
-            ),
-        )(queries, keys, values, cotangent, gain[None, :])
+            scratch_shapes=[pltpu.VMEM(full, F32)] * 2 + [pltpu.SemaphoreType.DMA((3,))],
+        )(*(pltpu.with_memory_space_constraint(b, pltpu.VMEM) for b in blocks))
     )
 
 

time: 60.8 us -> 56 us (0.921)
  local copies, waits for them, and re-layouts: 3.95 us -> 0 us
  Pallas kernels: 56 us -> 55.2 us
    unnamed x7 -> x0, local copies, waits for them, and re-layouts: 3.95 us -> none
    pallas_call x1 -> x2, Pallas kernels: 56 us -> 55.2 us  [the longest x1 53.6 us: shards(): pl.pallas_call(functools.partial(body, n_seq, n_head), out_shape=(pltpu.V...]
where the time goes in v2:
time: 56 us; the launch traced here: 55.9 us
  Pallas kernels  55.2 us (99%)
  between operations  0.64 us (1%)
    pallas_call x1, Pallas kernels, shards(): pl.pallas_call(functools.partial(body, n_seq, n_head), out_shape=(pltpu.V...  53.6 us
    pallas_call x1, Pallas kernels, shards(): pl.pallas_call(finish, out_shape=(out, out, out), in_specs=[vmem] * 9, ou...  1.59 us

profile of v2, /device:TPU:1, one launch (start us, length us, event | category | flops | bytes accessed | tf_op | source)
XLA Modules:
  0.0 55.9 jit_solution(11014856122327322984)
XLA Ops:
  0.6 53.6 %shard_map.76 = (f32[512,256]{1,0:T(8,128)S(1)}, f32[512,256]{1,0:T(8,128)S(1)}, f32[512,256]{1,0:T(8,128)S(1)}, bf16[512,256]{1,0:T(8,128)(2,1)S(1)}, bf16[512,...) custom-call(f32[512,256]{1,0:T(8,128)} %q_hbm.1, ...), custom_call_target="tpu_custom_call" | custom-call | tf_op jit(solution)/shard_map/pallas_call | solution.py:373
  54.3 1.6 %shard_map.77 = (f32[512,256]{1,0:T(8,128)}, f32[512,256]{1,0:T(8,128)}, f32[512,256]{1,0:T(8,128)}) custom-call(f32[512,256]{1,0:T(8,128)S(1)} %get-tuple-element.12.gq_s, f32[512,256]{1,0:T(8,128)S(1)} %get-tuple-element.13.gk_s, f32[512,256]{1,0:T(8,128)S(1)} %get-tuple-element.14.gv_s, bf16[512,256]{1,0:T(8,128)(2,1)S(1)} %get-tuple-element.15.kh, ...), custom_call_target="tpu_custom_call" | custom-call | tf_op jit(solution)/shard_map/pallas_call | solution.py:400

commit v3 on v2

--- a/solution.py
+++ b/solution.py
@@ -31,6 +31,15 @@
 
 def far_first(count):
     return sorted(range(1, count), key=lambda m: -min(m, count - m))
+
+
+def relay_steps(count):
+    known, steps = 1, []
+    while 2 * known + 1 < count:
+        step = min(known, count // 2 - known)
+        steps.append(step)
+        known += step
+    return steps
 
 
 NN = ((1,), (0,))
@@ -64,6 +73,8 @@
     ql,
     gh,
     gl,
+    qt_h,
+    qt_l,
     sco_h,
     sco_l,
     bd_h,
@@ -78,6 +89,8 @@
     in_sem,
     send_sem,
     recv_sem,
+    col_sem,
+    head_sem,
 ):
     n_y = n_seq // ROW
     tokens, width = q_s.shape
@@ -98,6 +111,15 @@
     def head_peer(m):
         return (s, lax.rem(h + m, n_head))
 
+    def near(count, peer):
+        return [peer(m) for m in sorted({1, count - 1}) if 0 < m < count]
+
+    barrier = pltpu.get_barrier_semaphore()
+    peers = (
+        [row_peer(k) for k in far_first(ROW)] + near(n_y, col_peer) + near(n_head, head_peer)
+    )
+    for peer in peers:
+        pl.semaphore_signal(barrier, inc=1, device_id=peer, device_id_type=MESH)
     loads = [
         pltpu.make_async_copy(src, dst, in_sem.at[i])
         for i, (src, dst) in enumerate(
@@ -106,14 +128,18 @@
     ]
     for load in loads:
         load.start()
-    barrier = pltpu.get_barrier_semaphore()
-    peers = (
-        [row_peer(k) for k in range(1, ROW)]
-        + [col_peer(m) for m in range(1, n_y)]
-        + [head_peer(m) for m in range(1, n_head)]
-    )
-    for peer in peers:
-        pl.semaphore_signal(barrier, inc=1, device_id=peer, device_id_type=MESH)
+
+    def relay_signal(sem, count, peer, number):
+        steps = relay_steps(count)
+        if number < len(steps):
+            for m in (steps[number], count - steps[number]):
+                pl.semaphore_signal(
+                    sem.at[number], inc=1, device_id=peer(m), device_id_type=MESH
+                )
+
+    def relay_wait(sem, count, number):
+        if number < len(relay_steps(count)):
+            pl.semaphore_wait(sem.at[number], 2)
 
     def send(src, dst, stage, peer):
         pltpu.make_async_remote_copy(
@@ -164,6 +190,8 @@
         for k in range(1, ROW):
             total = total + row_in[scan, k - 1]
         col_in[scan, n_y - 1] = total
+        if scan == 0:
+            relay_wait(col_sem, n_y, 1)
         for m in far_first(n_y):
             send(
                 col_in.at[scan, n_y - 1],
@@ -172,6 +200,21 @@
                 col_peer(m),
             )
 
+    def scan_within(scan):
+        for k in far_first(ROW) + [0]:
+            there = lax.rem(j + k, ROW)
+            value = jnp.zeros((part, HD), F32)
+            for r in range(ROW):
+                source = lax.rem(j - r + ROW, ROW)
+                inside = (source > there) if scan else (source < there)
+                piece = (
+                    row_in[scan, r - 1]
+                    if r
+                    else own[scan, pl.ds(pl.multiple_of(j * part, part), part)]
+                )
+                value = value + weight(inside) * piece
+            row_out[scan, k] = value
+
     def scan_back(scan):
         if n_y > 1:
             wait_in(col_in.at[scan, pl.ds(0, n_y - 1)], 3 * scan + 1)
@@ -179,25 +222,11 @@
         for m in range(1, n_y):
             inside = (y < m) if scan else (y >= m)
             base = base + weight(inside) * col_in[scan, m - 1]
-        mine = own[scan, pl.ds(pl.multiple_of(j * part, part), part)]
-        for k in far_first(ROW) + [0]:
-            there = lax.rem(j + k, ROW)
-            value = base
-            for r in range(ROW):
-                source = lax.rem(j - r + ROW, ROW)
-                inside = (source > there) if scan else (source < there)
-                piece = mine if r == 0 else row_in[scan, r - 1]
-                value = value + weight(inside) * piece
-            if k == 0:
-                state[scan, pl.ds(pl.multiple_of(j * part, part), part)] = value
-            else:
-                row_out[scan, k - 1] = value
-                send(
-                    row_out.at[scan, k - 1],
-                    state.at[scan, pl.ds(pl.multiple_of(j * part, part), part)],
-                    3 * scan + 2,
-                    row_peer(k),
-                )
+        here = pl.ds(pl.multiple_of(j * part, part), part)
+        for k in far_first(ROW):
+            row_out[scan, k] += base
+            send(row_out.at[scan, k], state.at[scan, here], 3 * scan + 2, row_peer(k))
+        state[scan, here] = row_out[scan, 0] + base
 
     def scan_end(scan):
         wait_in(state.at[scan, pl.ds(0, (ROW - 1) * part)], 3 * scan + 2)
@@ -238,6 +267,8 @@
             put_block_diagonal(c, total)
     own[0] = total
     pl.semaphore_wait(barrier, len(peers))
+    relay_signal(col_sem, n_y, col_peer, 0)
+    relay_signal(head_sem, n_head, head_peer, 0)
     scan_row(0)
 
     loads[2].wait()
@@ -248,9 +279,18 @@
                 pair(qh, ql, rows(c), cols(i)), pair(kh, kl, rows(c), cols(i)), NT
             )
             sco_h[c, i], sco_l[c, i] = split(jnp.where(lower, scores, 0.0))
+        if c == 0:
+            relay_wait(col_sem, n_y, 0)
+            relay_signal(col_sem, n_y, col_peer, 1)
+            relay_wait(head_sem, n_head, 0)
+            relay_signal(head_sem, n_head, head_peer, 1)
     loads[3].wait()
     sc_s[...] = sc_s[...] * gain_ref[...]
     scan_col(0)
+    relay_wait(head_sem, n_head, 1)
+    relay_signal(head_sem, n_head, head_peer, 2)
+    scan_within(0)
+    qt_h[...], qt_l[...] = split(q_s[...].T)
     for c in range(chunks):
         for i in range(heads):
             inner = dot3(pair(sco_h, sco_l, c, i), pair(vh, vl, rows(c), cols(i)), NN)
@@ -275,6 +315,7 @@
         sums = jnp.where(lane == g, squares[piece], sums)
         sums = jnp.where(lane == groups + g, cross[piece], sums)
     norm_own[...] = sums.T[: 2 * groups]
+    relay_wait(head_sem, n_head, 2)
     for m in far_first(n_head):
         send(norm_own, norm_in.at[m - 1], 6, head_peer(m))
     both = norm_own[...]
@@ -298,7 +339,9 @@
 
     total = jnp.zeros((heads * HD, HD), F32)
     for c in reversed(range(chunks)):
-        here = diagonal(dot3(pair(qh, ql, rows(c)), pair(gh, gl, rows(c)), TN))
+        here = diagonal(
+            dot3((qt_h[:, rows(c)], qt_l[:, rows(c)]), pair(gh, gl, rows(c)), NN)
+        )
         total = total + here
         if c > 0:
             put_block_diagonal(chunks + c, total)
@@ -323,6 +366,7 @@
 
     mix(0)
     scan_col(1)
+    scan_within(1)
     for c in range(1, chunks):
         mix(c)
     scan_back(1)
@@ -338,7 +382,7 @@
         wait_out(row_in.at[scan], 3 * scan)
         if n_y > 1:
             wait_out(col_in.at[scan, pl.ds(0, n_y - 1)], 3 * scan + 1)
-        wait_out(row_out.at[scan], 3 * scan + 2)
+        wait_out(row_out.at[scan, pl.ds(1, ROW - 1)], 3 * scan + 2)
     if n_head > 1:
         wait_out(norm_in, 6)
 
@@ -379,19 +423,22 @@
         out_specs=(vmem,) * 9,
         scratch_shapes=[pltpu.VMEM(full, F32)] * 5
         + [pltpu.VMEM(full, BF16)] * 4
+        + [pltpu.VMEM((width, tokens), BF16)] * 2
         + [pltpu.VMEM((chunks, heads, CHUNK, CHUNK), BF16)] * 2
         + [pltpu.VMEM((2 * chunks, width, width), BF16)] * 2
         + [
             pltpu.VMEM((2, heads * HD, HD), F32),
             pltpu.VMEM((2, ROW - 1, part, HD), F32),
             pltpu.VMEM((2, n_y, part, HD), F32),
-            pltpu.VMEM((2, ROW - 1, part, HD), F32),
+            pltpu.VMEM((2, ROW, part, HD), F32),
             pltpu.VMEM((2, heads * HD, HD), F32),
             pltpu.VMEM((norm_rows, HD), F32),
             pltpu.VMEM((max(n_head - 1, 1), norm_rows, HD), F32),
             pltpu.SemaphoreType.DMA((4,)),
             pltpu.SemaphoreType.DMA((7,)),
             pltpu.SemaphoreType.DMA((7,)),
+            pltpu.SemaphoreType.REGULAR((3,)),
+            pltpu.SemaphoreType.REGULAR((3,)),
         ],
         compiler_params=pltpu.CompilerParams(collective_id=0, has_side_effects=True),
     )(queries, keys, values, cotangent, gain[None, :])

time: 56 us -> 53.2 us (0.950)
  Pallas kernels: 55.2 us -> 52.4 us
    pallas_call x1, Pallas kernels: 53.6 us -> 50.8 us  [shards(): pl.pallas_call(functools.partial(body, n_seq, n_head), out_shape=(pltpu.V...]
where the time goes in v3:
time: 53.2 us; the launch traced here: 53 us
  Pallas kernels  52.4 us (98%)
  between operations  0.64 us (1%)
    pallas_call x1, Pallas kernels, shards(): pl.pallas_call(functools.partial(body, n_seq, n_head), out_shape=(pltpu.V...  50.8 us
    pallas_call x1, Pallas kernels, shards(): pl.pallas_call(finish, out_shape=(out, out, out), in_specs=[vmem] * 9, ou...  1.59 us

profile of v3, /device:TPU:1, one launch (start us, length us, event | category | flops | bytes accessed | tf_op | source)
XLA Modules:
  0.0 53.0 jit_solution(3254621752888379996)
XLA Ops:
  0.6 50.8 %shard_map.76 = (f32[512,256]{1,0:T(8,128)S(1)}, f32[512,256]{1,0:T(8,128)S(1)}, f32[512,256]{1,0:T(8,128)S(1)}, bf16[512,256]{1,0:T(8,128)(2,1)S(1)}, bf16[512,...) custom-call(f32[512,256]{1,0:T(8,128)} %q_hbm.1, ...), custom_call_target="tpu_custom_call" | custom-call | tf_op jit(solution)/shard_map/pallas_call | solution.py:417
  51.4 1.6 %shard_map.77 = (f32[512,256]{1,0:T(8,128)}, f32[512,256]{1,0:T(8,128)}, f32[512,256]{1,0:T(8,128)}) custom-call(f32[512,256]{1,0:T(8,128)S(1)} %get-tuple-element.12.gq_s, f32[512,256]{1,0:T(8,128)S(1)} %get-tuple-element.13.gk_s, f32[512,256]{1,0:T(8,128)S(1)} %get-tuple-element.14.gv_s, bf16[512,256]{1,0:T(8,128)(2,1)S(1)} %get-tuple-element.15.kh, ...), custom_call_target="tpu_custom_call" | custom-call | tf_op jit(solution)/shard_map/pallas_call | solution.py:447

commit v4 on v3

--- a/solution.py
+++ b/solution.py
@@ -33,6 +33,10 @@
     return sorted(range(1, count), key=lambda m: -min(m, count - m))
 
 
+def row_order(count):
+    return sorted(range(1, count), key=lambda k: -(min(k, count - k) + 1.5 * (k % 2)))
+
+
 def relay_steps(count):
     known, steps = 1, []
     while 2 * known + 1 < count:
@@ -54,7 +58,7 @@
     k_hbm,
     v_hbm,
     cot_hbm,
-    gain_ref,
+    gain_hbm,
     gq_s,
     gk_s,
     gv_s,
@@ -68,6 +72,7 @@
     k_s,
     v_s,
     sc_s,
+    gain_s,
     att_s,
     qh,
     ql,
@@ -89,6 +94,8 @@
     in_sem,
     send_sem,
     recv_sem,
+    col_send,
+    col_recv,
     col_sem,
     head_sem,
 ):
@@ -116,14 +123,14 @@
 
     barrier = pltpu.get_barrier_semaphore()
     peers = (
-        [row_peer(k) for k in far_first(ROW)] + near(n_y, col_peer) + near(n_head, head_peer)
+        [row_peer(k) for k in row_order(ROW)] + near(n_y, col_peer) + near(n_head, head_peer)
     )
     for peer in peers:
         pl.semaphore_signal(barrier, inc=1, device_id=peer, device_id_type=MESH)
     loads = [
         pltpu.make_async_copy(src, dst, in_sem.at[i])
         for i, (src, dst) in enumerate(
-            [(k_hbm, k_s), (v_hbm, v_s), (q_hbm, q_s), (cot_hbm, sc_s)]
+            [(k_hbm, k_s), (v_hbm, v_s), (q_hbm, q_s), (cot_hbm, sc_s), (gain_hbm, gain_s)]
         )
     ]
     for load in loads:
@@ -141,51 +148,57 @@
         if number < len(relay_steps(count)):
             pl.semaphore_wait(sem.at[number], 2)
 
-    def send(src, dst, stage, peer):
-        pltpu.make_async_remote_copy(
+    def remote(src, dst, sems, peer):
+        return pltpu.make_async_remote_copy(
             src_ref=src,
             dst_ref=dst,
-            send_sem=send_sem.at[stage],
-            recv_sem=recv_sem.at[stage],
+            send_sem=sems[0],
+            recv_sem=sems[1],
             device_id=peer,
             device_id_type=MESH,
-        ).start()
+        )
+
+    def sems(stage):
+        return send_sem.at[stage], recv_sem.at[stage]
+
+    def send(src, dst, stage, peer):
+        remote(src, dst, sems(stage), peer).start()
 
     def wait_in(ref, stage):
-        pltpu.make_async_remote_copy(
-            src_ref=ref,
-            dst_ref=ref,
-            send_sem=send_sem.at[stage],
-            recv_sem=recv_sem.at[stage],
-            device_id=row_peer(1),
-            device_id_type=MESH,
-        ).wait_recv()
+        remote(ref, ref, sems(stage), row_peer(1)).wait_recv()
 
     def wait_out(ref, stage):
-        pltpu.make_async_remote_copy(
-            src_ref=ref,
-            dst_ref=ref,
-            send_sem=send_sem.at[stage],
-            recv_sem=recv_sem.at[stage],
-            device_id=row_peer(1),
-            device_id_type=MESH,
-        ).wait_send()
+        remote(ref, ref, sems(stage), row_peer(1)).wait_send()
+
+    def col_copy(scan, m):
+        return remote(
+            col_in.at[scan, n_y - 1],
+            col_in.at[scan, m - 1],
+            (col_send.at[scan, m - 1], col_recv.at[scan, m - 1]),
+            col_peer(m),
+        )
+
+    def goes(scan, m):
+        return (y + m >= n_y) if scan else (y + m < n_y)
+
+    def comes(scan, m):
+        return (y < m) if scan else (y >= m)
 
     def weight(cond):
         return jnp.where(cond, 1.0, 0.0).astype(F32)
 
     def scan_row(scan):
-        for k in far_first(ROW):
+        for k in row_order(ROW):
             there = lax.rem(j + k, ROW)
             send(
                 own.at[scan, pl.ds(pl.multiple_of(there * part, part), part)],
                 row_in.at[scan, k - 1],
-                3 * scan,
+                2 * scan,
                 row_peer(k),
             )
 
     def scan_col(scan):
-        wait_in(row_in.at[scan], 3 * scan)
+        wait_in(row_in.at[scan], 2 * scan)
         total = own[scan, pl.ds(pl.multiple_of(j * part, part), part)]
         for k in range(1, ROW):
             total = total + row_in[scan, k - 1]
@@ -193,15 +206,13 @@
         if scan == 0:
             relay_wait(col_sem, n_y, 1)
         for m in far_first(n_y):
-            send(
-                col_in.at[scan, n_y - 1],
-                col_in.at[scan, m - 1],
-                3 * scan + 1,
-                col_peer(m),
-            )
+
+            @pl.when(goes(scan, m))
+            def _():
+                col_copy(scan, m).start()
 
     def scan_within(scan):
-        for k in far_first(ROW) + [0]:
+        for k in row_order(ROW) + [0]:
             there = lax.rem(j + k, ROW)
             value = jnp.zeros((part, HD), F32)
             for r in range(ROW):
@@ -216,20 +227,23 @@
             row_out[scan, k] = value
 
     def scan_back(scan):
-        if n_y > 1:
-            wait_in(col_in.at[scan, pl.ds(0, n_y - 1)], 3 * scan + 1)
+        for m in range(1, n_y):
+
+            @pl.when(comes(scan, m))
+            def _():
+                col_copy(scan, m).wait_recv()
+
         base = jnp.zeros((part, HD), F32)
         for m in range(1, n_y):
-            inside = (y < m) if scan else (y >= m)
-            base = base + weight(inside) * col_in[scan, m - 1]
+            base = base + jnp.where(comes(scan, m), col_in[scan, m - 1], 0.0)
         here = pl.ds(pl.multiple_of(j * part, part), part)
-        for k in far_first(ROW):
+        for k in row_order(ROW):
             row_out[scan, k] += base
-            send(row_out.at[scan, k], state.at[scan, here], 3 * scan + 2, row_peer(k))
+            send(row_out.at[scan, k], state.at[scan, here], 2 * scan + 1, row_peer(k))
         state[scan, here] = row_out[scan, 0] + base
 
     def scan_end(scan):
-        wait_in(state.at[scan, pl.ds(0, (ROW - 1) * part)], 3 * scan + 2)
+        wait_in(state.at[scan, pl.ds(0, (ROW - 1) * part)], 2 * scan + 1)
 
     def cols(head):
         return slice(head * HD, (head + 1) * HD)
@@ -285,7 +299,8 @@
             relay_wait(head_sem, n_head, 0)
             relay_signal(head_sem, n_head, head_peer, 1)
     loads[3].wait()
-    sc_s[...] = sc_s[...] * gain_ref[...]
+    loads[4].wait()
+    sc_s[...] = sc_s[...] * gain_s[...]
     scan_col(0)
     relay_wait(head_sem, n_head, 1)
     relay_signal(head_sem, n_head, head_peer, 2)
@@ -317,10 +332,10 @@
     norm_own[...] = sums.T[: 2 * groups]
     relay_wait(head_sem, n_head, 2)
     for m in far_first(n_head):
-        send(norm_own, norm_in.at[m - 1], 6, head_peer(m))
+        send(norm_own, norm_in.at[m - 1], 4, head_peer(m))
     both = norm_own[...]
     if n_head > 1:
-        wait_in(norm_in, 6)
+        wait_in(norm_in, 4)
         for m in range(1, n_head):
             both = both + norm_in[m - 1]
     mean = both / (width * n_head)
@@ -379,29 +394,37 @@
         after_h[cols(i), cols(i)] = high[cols(i)]
         after_l[cols(i), cols(i)] = low[cols(i)]
     for scan in range(2):
-        wait_out(row_in.at[scan], 3 * scan)
-        if n_y > 1:
-            wait_out(col_in.at[scan, pl.ds(0, n_y - 1)], 3 * scan + 1)
-        wait_out(row_out.at[scan, pl.ds(1, ROW - 1)], 3 * scan + 2)
+        wait_out(row_in.at[scan], 2 * scan)
+        for m in range(1, n_y):
+
+            @pl.when(goes(scan, m))
+            def _():
+                col_copy(scan, m).wait_send()
+
+        wait_out(row_out.at[scan, pl.ds(1, ROW - 1)], 2 * scan + 1)
     if n_head > 1:
-        wait_out(norm_in, 6)
+        wait_out(norm_in, 4)
 
 
 def finish(
     gq_s, gk_s, gv_s, kh, kl, vh, vl, after_h, after_l, gq_hbm, gk_hbm, gv_hbm, k_out, v_out, sem
 ):
     after = (after_h[...], after_l[...])
-    stores = [
-        pltpu.make_async_copy(src, dst, sem.at[i])
-        for i, (src, dst) in enumerate([(gq_s, gq_hbm), (k_out, gk_hbm), (v_out, gv_hbm)])
-    ]
+    stores = [pltpu.make_async_copy(gq_s, gq_hbm, sem.at[0])]
     stores[0].start()
-    k_out[...] = gk_s[...] + dot3((vh[...], vl[...]), after, NT)
-    stores[1].start()
-    v_out[...] = gv_s[...] + dot3((kh[...], kl[...]), after, NN)
-    stores[2].start()
-    for store in stores:
-        store.wait()
+
+    def store(src, dst, piece):
+        stores.append(pltpu.make_async_copy(src.at[piece], dst.at[piece], sem.at[len(stores)]))
+        stores[-1].start()
+
+    for c in range(gq_s.shape[0] // CHUNK):
+        piece = pl.ds(c * CHUNK, CHUNK)
+        k_out[piece] = gk_s[piece] + dot3((vh[piece], vl[piece]), after, NT)
+        store(k_out, gk_hbm, piece)
+        v_out[piece] = gv_s[piece] + dot3((kh[piece], kl[piece]), after, NN)
+        store(v_out, gv_hbm, piece)
+    for copy in stores:
+        copy.wait()
 
 
 def shards(n_seq, n_head, queries, keys, values, cotangent, gain):
@@ -419,9 +442,10 @@
         out_shape=(pltpu.VMEM(full, F32),) * 3
         + (pltpu.VMEM(full, BF16),) * 4
         + (pltpu.VMEM((width, width), BF16),) * 2,
-        in_specs=[anywhere] * 4 + [vmem],
+        in_specs=[anywhere] * 5,
         out_specs=(vmem,) * 9,
-        scratch_shapes=[pltpu.VMEM(full, F32)] * 5
+        scratch_shapes=[pltpu.VMEM(full, F32)] * 4
+        + [pltpu.VMEM((1, width), F32), pltpu.VMEM(full, F32)]
         + [pltpu.VMEM(full, BF16)] * 4
         + [pltpu.VMEM((width, tokens), BF16)] * 2
         + [pltpu.VMEM((chunks, heads, CHUNK, CHUNK), BF16)] * 2
@@ -434,9 +458,11 @@
             pltpu.VMEM((2, heads * HD, HD), F32),
             pltpu.VMEM((norm_rows, HD), F32),
             pltpu.VMEM((max(n_head - 1, 1), norm_rows, HD), F32),
-            pltpu.SemaphoreType.DMA((4,)),
-            pltpu.SemaphoreType.DMA((7,)),
-            pltpu.SemaphoreType.DMA((7,)),
+            pltpu.SemaphoreType.DMA((5,)),
+            pltpu.SemaphoreType.DMA((5,)),
+            pltpu.SemaphoreType.DMA((5,)),
+            pltpu.SemaphoreType.DMA((2, max(n_y - 1, 1))),
+            pltpu.SemaphoreType.DMA((2, max(n_y - 1, 1))),
             pltpu.SemaphoreType.REGULAR((3,)),
             pltpu.SemaphoreType.REGULAR((3,)),
         ],
@@ -449,7 +475,7 @@
             out_shape=(out, out, out),
             in_specs=[vmem] * 9,
             out_specs=(anywhere,) * 3,
-            scratch_shapes=[pltpu.VMEM(full, F32)] * 2 + [pltpu.SemaphoreType.DMA((3,))],
+            scratch_shapes=[pltpu.VMEM(full, F32)] * 2 + [pltpu.SemaphoreType.DMA((1 + 2 * chunks,))],
         )(*(pltpu.with_memory_space_constraint(b, pltpu.VMEM) for b in blocks))
     )
 

time: 53.2 us -> 51.9 us (0.976)
  Pallas kernels: 52.4 us -> 51.2 us
    pallas_call x1, Pallas kernels: 50.8 us -> 49.8 us  [shards(): pl.pallas_call(functools.partial(body, n_seq, n_head), out_shape=(pltpu.V...]
where the time goes in v4:
time: 51.9 us; the launch traced here: 51.8 us
  Pallas kernels  51.2 us (99%)
  between operations  0.64 us (1%)
    pallas_call x1, Pallas kernels, shards(): pl.pallas_call(functools.partial(body, n_seq, n_head), out_shape=(pltpu.V...  49.8 us
    pallas_call x1, Pallas kernels, shards(): pl.pallas_call(finish, out_shape=(out, out, out), in_specs=[vmem] * 9, ou...  1.4 us

profile of v4, /device:TPU:1, one launch (start us, length us, event | category | flops | bytes accessed | tf_op | source)
XLA Modules:
  0.0 51.8 jit_solution(950595058042428755)
XLA Ops:
  0.6 49.8 %shard_map.76 = (f32[512,256]{1,0:T(8,128)S(1)}, f32[512,256]{1,0:T(8,128)S(1)}, f32[512,256]{1,0:T(8,128)S(1)}, bf16[512,256]{1,0:T(8,128)(2,1)S(1)}, bf16[512,...) custom-call(f32[512,256]{1,0:T(8,128)} %q_hbm.1, ...), custom_call_target="tpu_custom_call" | custom-call | tf_op jit(solution)/shard_map/pallas_call | solution.py:440
  50.4 1.4 %shard_map.77 = (f32[512,256]{1,0:T(8,128)}, f32[512,256]{1,0:T(8,128)}, f32[512,256]{1,0:T(8,128)}) custom-call(f32[512,256]{1,0:T(8,128)S(1)} %get-tuple-element.12.gq_s, f32[512,256]{1,0:T(8,128)S(1)} %get-tuple-element.13.gk_s, f32[512,256]{1,0:T(8,128)S(1)} %get-tuple-element.14.gv_s, bf16[512,256]{1,0:T(8,128)(2,1)S(1)} %get-tuple-element.15.kh, ...), custom_call_target="tpu_custom_call" | custom-call | tf_op jit(solution)/shard_map/pallas_call | solution.py:473

commit v5 on v4

--- a/solution.py
+++ b/solution.py
@@ -227,20 +227,27 @@
             row_out[scan, k] = value
 
     def scan_back(scan):
-        for m in range(1, n_y):
+        base = jnp.zeros((part, HD), F32)
+        for m in reversed(far_first(n_y)):
 
             @pl.when(comes(scan, m))
             def _():
                 col_copy(scan, m).wait_recv()
 
-        base = jnp.zeros((part, HD), F32)
-        for m in range(1, n_y):
             base = base + jnp.where(comes(scan, m), col_in[scan, m - 1], 0.0)
         here = pl.ds(pl.multiple_of(j * part, part), part)
         for k in row_order(ROW):
             row_out[scan, k] += base
             send(row_out.at[scan, k], state.at[scan, here], 2 * scan + 1, row_peer(k))
         state[scan, here] = row_out[scan, 0] + base
+
+    def sent(scan):
+        wait_out(row_in.at[scan], 2 * scan)
+        for m in range(1, n_y):
+
+            @pl.when(goes(scan, m))
+            def _():
+                col_copy(scan, m).wait_send()
 
     def scan_end(scan):
         wait_in(state.at[scan, pl.ds(0, (ROW - 1) * part)], 2 * scan + 1)
@@ -321,14 +328,15 @@
     lane = lax.broadcasted_iota(jnp.int32, (HD, HD), 1)
     groups = tokens // HD
     sums = jnp.zeros((HD, HD), F32)
-    att = att_s[...] + dot3((qh[...], ql[...]), pair(bd_h, bd_l, chunks), NN)
-    att_s[...] = att
-    squares = jnp.sum(att * att, axis=1, keepdims=True)
-    cross = jnp.sum(att * sc_s[...], axis=1, keepdims=True)
+    before = pair(bd_h, bd_l, chunks)
     for g in range(groups):
         piece = slice(g * HD, (g + 1) * HD)
-        sums = jnp.where(lane == g, squares[piece], sums)
-        sums = jnp.where(lane == groups + g, cross[piece], sums)
+        att = att_s[piece] + dot3(pair(qh, ql, piece), before, NN)
+        att_s[piece] = att
+        squares = jnp.sum(att * att, axis=1, keepdims=True)
+        cross = jnp.sum(att * sc_s[piece], axis=1, keepdims=True)
+        sums = jnp.where(lane == g, squares, sums)
+        sums = jnp.where(lane == groups + g, cross, sums)
     norm_own[...] = sums.T[: 2 * groups]
     relay_wait(head_sem, n_head, 2)
     for m in far_first(n_head):
@@ -384,26 +392,21 @@
     scan_within(1)
     for c in range(1, chunks):
         mix(c)
-    scan_back(1)
-    scan_end(1)
-
+    sent(0)
+    wait_out(row_out.at[0, pl.ds(1, ROW - 1)], 1)
+    if n_head > 1:
+        wait_out(norm_in, 4)
     after_h[...] = jnp.zeros_like(after_h)
     after_l[...] = jnp.zeros_like(after_l)
+    scan_back(1)
+    sent(1)
+    scan_end(1)
+
     high, low = split(state[1])
     for i in range(heads):
         after_h[cols(i), cols(i)] = high[cols(i)]
         after_l[cols(i), cols(i)] = low[cols(i)]
-    for scan in range(2):
-        wait_out(row_in.at[scan], 2 * scan)
-        for m in range(1, n_y):
-
-            @pl.when(goes(scan, m))
-            def _():
-                col_copy(scan, m).wait_send()
-
-        wait_out(row_out.at[scan, pl.ds(1, ROW - 1)], 2 * scan + 1)
-    if n_head > 1:
-        wait_out(norm_in, 4)
+    wait_out(row_out.at[1, pl.ds(1, ROW - 1)], 3)
 
 
 def finish(

time: 51.9 us -> 51.7 us (level)
  no operation moved by 1% of the time
where the time goes in v5:
time: 51.7 us; the launch traced here: 51.6 us
  Pallas kernels  50.9 us (98%)
  between operations  0.64 us (1%)
    pallas_call x1, Pallas kernels, shards(): pl.pallas_call(functools.partial(body, n_seq, n_head), out_shape=(pltpu.V...  49.5 us
    pallas_call x1, Pallas kernels, shards(): pl.pallas_call(finish, out_shape=(out, out, out), in_specs=[vmem] * 9, ou...  1.4 us

profile of v5, /device:TPU:1, one launch (start us, length us, event | category | flops | bytes accessed | tf_op | source)
XLA Modules:
  0.0 51.6 jit_solution(3459969442848498290)
XLA Ops:
  0.6 49.5 %shard_map.76 = (f32[512,256]{1,0:T(8,128)S(1)}, f32[512,256]{1,0:T(8,128)S(1)}, f32[512,256]{1,0:T(8,128)S(1)}, bf16[512,256]{1,0:T(8,128)(2,1)S(1)}, bf16[512,...) custom-call(f32[512,256]{1,0:T(8,128)} %q_hbm.1, ...), custom_call_target="tpu_custom_call" | custom-call | tf_op jit(solution)/shard_map/pallas_call | solution.py:443
  50.2 1.4 %shard_map.77 = (f32[512,256]{1,0:T(8,128)}, f32[512,256]{1,0:T(8,128)}, f32[512,256]{1,0:T(8,128)}) custom-call(f32[512,256]{1,0:T(8,128)S(1)} %get-tuple-element.12.gq_s, f32[512,256]{1,0:T(8,128)S(1)} %get-tuple-element.13.gk_s, f32[512,256]{1,0:T(8,128)S(1)} %get-tuple-element.14.gv_s, bf16[512,256]{1,0:T(8,128)(2,1)S(1)} %get-tuple-element.15.kh, ...), custom_call_target="tpu_custom_call" | custom-call | tf_op jit(solution)/shard_map/pallas_call | solution.py:476

commit v6 on v5

--- a/solution.py
+++ b/solution.py
@@ -22,11 +22,14 @@
 
 
 def dot3(left, right, dims):
-    def one(a, b):
-        return lax.dot_general(a, b, (dims, ((), ())), preferred_element_type=F32)
-
     (lh, ll), (rh, rl) = left, right
-    return one(lh, rh) + (one(lh, rl) + one(ll, rh))
+    (lc,), (rc,) = dims
+    return lax.dot_general(
+        jnp.concatenate([lh, lh, ll], axis=lc),
+        jnp.concatenate([rh, rl, rh], axis=rc),
+        (dims, ((), ())),
+        preferred_element_type=F32,
+    )
 
 
 def far_first(count):

time: 51.7 us -> 51.7 us (level)
  no operation moved by 1% of the time
where the time goes in v6:
time: 51.7 us; the launch traced here: 51.5 us
  Pallas kernels  50.9 us (98%)
  between operations  0.64 us (1%)
    pallas_call x1, Pallas kernels, shards(): pl.pallas_call(functools.partial(body, n_seq, n_head), out_shape=(pltpu.V...  49.5 us
    pallas_call x1, Pallas kernels, shards(): pl.pallas_call(finish, out_shape=(out, out, out), in_specs=[vmem] * 9, ou...  1.4 us

profile of v6, /device:TPU:1, one launch (start us, length us, event | category | flops | bytes accessed | tf_op | source)
XLA Modules:
  0.0 51.5 jit_solution(13196151001164448513)
XLA Ops:
  0.6 49.5 %shard_map.76 = (f32[512,256]{1,0:T(8,128)S(1)}, f32[512,256]{1,0:T(8,128)S(1)}, f32[512,256]{1,0:T(8,128)S(1)}, bf16[512,256]{1,0:T(8,128)(2,1)S(1)}, bf16[512,...) custom-call(f32[512,256]{1,0:T(8,128)} %q_hbm.1, ...), custom_call_target="tpu_custom_call" | custom-call | tf_op jit(solution)/shard_map/pallas_call | solution.py:446
  50.1 1.4 %shard_map.77 = (f32[512,256]{1,0:T(8,128)}, f32[512,256]{1,0:T(8,128)}, f32[512,256]{1,0:T(8,128)}) custom-call(f32[512,256]{1,0:T(8,128)S(1)} %get-tuple-element.12.gq_s, f32[512,256]{1,0:T(8,128)S(1)} %get-tuple-element.13.gk_s, f32[512,256]{1,0:T(8,128)S(1)} %get-tuple-element.14.gv_s, bf16[512,256]{1,0:T(8,128)(2,1)S(1)} %get-tuple-element.15.kh, ...), custom_call_target="tpu_custom_call" | custom-call | tf_op jit(solution)/shard_map/pallas_call | solution.py:479
